TPU v7x, 32 devices: a whole 2x2x4 slice. The times are simulated.
32 devices in a mesh: fsdp: 4 (over y, x), grp: 8 (over z, core).
Axes of the slice: x: 2, y: 2, z: 4, core: 2. Of those that a mesh axis runs over, the one named last changes fastest.
Arguments:
- grad_out: bfloat16 [32, 512, 512], P(('fsdp', 'grp')), may hold values from -6 to 6
- pre_first: bfloat16 [32, 512, 512], P(('fsdp', 'grp')), may hold values from -8 to 8
- pre_second: bfloat16 [32, 512, 512], P(('fsdp', 'grp')), may hold values from -8 to 8
- conv_first: bfloat16 [3, 512, 512], P(None, 'fsdp'), may hold values from -0.15625 to 0.15625
- conv_second: bfloat16 [3, 512, 512], P(None, 'fsdp'), may hold values from -0.15625 to 0.15625
- lengths: int32 [32], P(('fsdp', 'grp')), may hold values from 64 to 512
- item_ids: int32 [16384], P('grp'), may hold values from 0 to 8191
- owners: int32 [512, 1], P('grp'), may hold values from 0 to 7; in each aligned block of 64 rows (0 to 63, 64 to 127, ...) at most 16 rows name the same one
Outputs:
- table_grad: float32 [512, 65536], P('fsdp', 'grp')
Inputs may be any that keep to these rules, and one draw needn't show every extreme that they name: `owners`: among the blocks of one group, no owner is named by more than 16 blocks, a bound that some block reaches.
All inputs are finite; a program needn't handle non-finite values.
Results may differ from a plain program's by a relative error of at most 0.0037.
Values may be sent and summed in bfloat16 or wider, within the bound.
A program may use at most 64 MiB of HBM per device.

v0:
```python
import jax
import jax.numpy as jnp
from jax import lax
from jax.sharding import PartitionSpec as P

BLK = 32
ROWS_OWN = 8192


def layer_back(gradient, pre_acts, live_rows, dilation, product):
    seq_len = gradient.shape[0]
    pre_float = pre_acts.astype(jnp.float32)
    sig_val = jax.nn.sigmoid(pre_float)
    deltas = (gradient * sig_val * (1.0 + pre_float * (1.0 - sig_val))).astype(jnp.bfloat16)
    padded = jnp.pad(deltas, ((dilation, dilation), (0, 0)))
    tap_rows = jnp.stack(
        [
            padded[2 * dilation : 2 * dilation + seq_len],
            padded[dilation : dilation + seq_len],
            padded[0:seq_len],
        ]
    )
    return gradient + live_rows * product(tap_rows)


def gathered_product(weights):

    def apply_taps(tap_rows):
        return jnp.einsum(
            "ktd,kpd->tp",
            tap_rows,
            lax.all_gather(weights, "fsdp", axis=1, tiled=True),
            preferred_element_type=jnp.float32,
        )

    return apply_taps


def body(grad_out, pre_first, pre_second, conv_first, conv_second, lengths, item_ids, owners):
    seq_len = grad_out.shape[1]
    positions = jnp.arange(seq_len, dtype=jnp.int32)
    live_rows = (positions < lengths[0]).astype(jnp.float32)[:, None]
    gradient = grad_out[0].astype(jnp.float32)
    gradient = layer_back(gradient, pre_second[0], live_rows, 2, gathered_product(conv_second))
    gradient = layer_back(gradient, pre_first[0], live_rows, 1, gathered_product(conv_first))
    row_grad = (live_rows * gradient).astype(jnp.bfloat16)
    group_cols = lax.all_to_all(row_grad.T, "fsdp", split_axis=0, concat_axis=1, tiled=True)
    feat_cols = group_cols.shape[0]
    owner_count = lax.axis_size("grp")
    blocks = owners.shape[0]
    slot_cap = max(2, 2 * blocks // owner_count)
    block_dest = owners[:, 0]
    dest_hits = (block_dest[:, None] == jnp.arange(owner_count, dtype=jnp.int32)[None, :]).astype(
        jnp.int32
    )
    earlier = jnp.cumsum(dest_hits, axis=0) - dest_hits
    block_rank = jnp.sum(dest_hits * earlier, axis=1)
    slot_index = block_dest * slot_cap + block_rank
    select_int = (
        slot_index[:, None] == jnp.arange(owner_count * slot_cap, dtype=jnp.int32)[None, :]
    ).astype(jnp.int32)
    select_int = select_int.reshape(blocks, owner_count, slot_cap)
    select_map = select_int.astype(jnp.bfloat16)
    block_cols = group_cols.reshape(feat_cols, blocks, BLK)
    send_rows = jnp.einsum(
        "cbr,bos->ocsr", block_cols, select_map, preferred_element_type=jnp.float32
    )
    send_rows = send_rows.astype(jnp.bfloat16).reshape(owner_count, feat_cols, slot_cap * BLK)
    shifted_ids = item_ids.reshape(blocks, BLK) + 1
    send_ids = jnp.einsum("br,bos->osr", shifted_ids, select_int) - 1
    send_ids = send_ids.reshape(owner_count, slot_cap * BLK)
    recv_rows, recv_ids = (
        lax.all_to_all(send_rows, "grp", split_axis=0, concat_axis=0, tiled=True),
        lax.all_to_all(send_ids, "grp", split_axis=0, concat_axis=0, tiled=True),
    )
    flat_rows = jnp.transpose(recv_rows, (0, 2, 1)).reshape(-1, feat_cols).astype(jnp.float32)
    safe_ids = jnp.where(recv_ids < 0, ROWS_OWN, recv_ids).reshape(-1)
    summed = jax.ops.segment_sum(flat_rows, safe_ids, num_segments=ROWS_OWN + 1)
    return summed[:ROWS_OWN].T


def solution(mesh):
    placed = (
        P(("fsdp", "grp"), None, None),
        P(("fsdp", "grp"), None, None),
        P(("fsdp", "grp"), None, None),
        P(None, "fsdp", None),
        P(None, "fsdp", None),
        P(("fsdp", "grp")),
        P("grp"),
        P("grp", None),
    )
    return jax.shard_map(
        body, mesh=mesh, in_specs=placed, out_specs=P("fsdp", "grp"), check_vma=False
    )
```

profile of v0, /device:TPU:0, one launch (start us, length us, event | category | flops | bytes accessed | tf_op | source)
XLA Modules:
  0.0 175.9 jit_solution(7663716986740653124)
XLA Ops:
  6.5 0.7 all-gather.3.cloned.1.call-update
  7.3 0.7 all-gather.5.cloned.1.call-update
  8.7 0.7 fusion.74
  9.5 0.8 select_reduce_fusion
  10.4 1.7 fusion.46
  12.4 0.5 fusion.48
  12.8 30.0 %all-gather.3.cloned.1.call-done = bf16[3,512,512]{2,1,0:T(8,128)(2,1)} async-done(((bf16[3,128,512]{2,1,0:T(8,128)(2,1)}), bf16[3,512,512]{2,1,0:T(8,128)(2,1)}) %all-gather.3.cloned.1.call-update) | async-done | bytes 1572880 | tf_op jit(solution)/shard_map/all_gather | solution.py:32
  42.8 3.7 %fusion.54 = (bf16[512,512]{1,0:T(8,128)(2,1)S(1)}, f32[512,512]{1,0:T(8,128)}) fusion(bf16[1,512,512]{2,1,0:T(8,128)(2,1)S(1)} %copy-done.4, bf16[3,512,512]{2,1,0:T(8,128)(2,1)} %all-gather.3.cloned.1.call-done, bf16[1,512,512]{2,1,0:T(8,128)(2,1)S(1)} %get-tuple-element.8, bf16[1,512,512]{2,1,0:T(8,128)(2,1)S(1)} %fusion.48, ...), kind=kOutput, calls=%fused_computation.47 | convolution fusion | flops 810287104 | bytes 5769216 | tf_op jit(solution)/shard_map/ktd,kpd->tp/dot_general | solution.py:29
  46.7 28.8 %all-gather.5.cloned.1.call-done = bf16[3,512,512]{2,1,0:T(8,128)(2,1)} async-done(((bf16[3,128,512]{2,1,0:T(8,128)(2,1)}), bf16[3,512,512]{2,1,0:T(8,128)(2,1)}) %all-gather.5.cloned.1.call-update) | async-done | bytes 1572880 | tf_op jit(solution)/shard_map/all_gather | solution.py:32
  75.5 2.4 %fusion.42 = bf16[64,4,8,128]{3,2,1,0:T(8,128)(2,1)S(1)} fusion(f32[512,512]{1,0:T(8,128)S(1)} %copy-done.5, bf16[3,512,512]{2,1,0:T(8,128)(2,1)} %all-gather.5.cloned.1.call-done, bf16[1,512,512]{2,1,0:T(8,128)(2,1)S(1)} %get-tuple-element.6, bf16[1,512,512]{2,1,0:T(8,128)(2,1)S(1)} %bitcast.101, bf16[1,512,512]{2,1,0:T(8,128)(2,1)S(1)} %get-tuple-element.5, ...), kind=kOutput, calls=%fused_computation.36 | convolution fusion | flops 807927808 | bytes 4720640 | tf_op jit(solution)/shard_map/ktd,kpd->tp/dot_general | solution.py:29
  77.9 0.9 copy.34
  78.8 3.5 %all-to-all-start.1 = ((bf16[4,128,512]{1,2,0:T(8,128)(2,1)}), bf16[4,128,512]{1,2,0:T(8,128)(2,1)S(1)}, u32[]{:S(2)}, u32[]{:S(2)}) async-start(bf16[4,128,512]{1,2,0:T(8,128)(2,1)} %bitcast.97), calls=%async_computation.1 | async-start | bytes 1048576 | tf_op jit(solution)/shard_map/all_to_all | solution.py:47
  82.4 0.2 convolution_add_fusion
  82.6 0.7 all_to_all.30
  83.3 7.1 %all-to-all-done.1 = bf16[4,128,512]{1,2,0:T(8,128)(2,1)S(1)} async-done(((bf16[4,128,512]{1,2,0:T(8,128)(2,1)}), bf16[4,128,512]{1,2,0:T(8,128)(2,1)S(1)}, u32[]{:S(2)}, u32[]{:S(2)}) %all-to-all-start.1) | async-done | bytes 524320 | tf_op jit(solution)/shard_map/all_to_all | solution.py:47
  90.4 4.6 %all-to-all-start = ((s32[8,1,512]{2,1,0:T(1,128)}), s32[8,1,512]{2,1,0:T(1,128)S(1)}, u32[]{:S(2)}, u32[]{:S(2)}) async-start(s32[8,1,512]{2,1,0:T(1,128)} %all_to_all.30), calls=%async_computation | async-start | bytes 32768 | tf_op jit(solution)/shard_map/all_to_all | solution.py:74
  95.0 0.5 fusion.14
  95.5 1.2 copy.21
  96.7 3.9 %all-to-all-done = s32[8,1,512]{2,1,0:T(1,128)S(1)} async-done(((s32[8,1,512]{2,1,0:T(1,128)}), s32[8,1,512]{2,1,0:T(1,128)S(1)}, u32[]{:S(2)}, u32[]{:S(2)}) %all-to-all-start) | async-done | bytes 16416 | tf_op jit(solution)/shard_map/all_to_all | solution.py:74
  100.7 3.6 %all-to-all-start.2 = ((bf16[8,128,512]{1,2,0:T(8,128)(2,1)}), bf16[8,128,512]{1,2,0:T(8,128)(2,1)S(1)}, u32[]{:S(2)}, u32[]{:S(2)}) async-start(bf16[8,128,512]{1,2,0:T(8,128)(2,1)} %bitcast.25), calls=%async_computation.2 | async-start | bytes 2097152 | tf_op jit(solution)/shard_map/all_to_all | solution.py:73
  104.2 26.5 %all-to-all-done.2 = bf16[8,128,512]{1,2,0:T(8,128)(2,1)S(1)} async-done(((bf16[8,128,512]{1,2,0:T(8,128)(2,1)}), bf16[8,128,512]{1,2,0:T(8,128)(2,1)S(1)}, u32[]{:S(2)}, u32[]{:S(2)}) %all-to-all-start.2) | async-done | bytes 1048608 | tf_op jit(solution)/shard_map/all_to_all | solution.py:73
  130.9 28.2 %scatter_custom_fusion = f32[8193,128]{1,0:T(8,128)} fusion(s32[4096]{0:T(1024)S(1)} %bitcast.103, f32[4096,128]{1,0:T(8,128)S(1)} %bitcast.99, f32[]{:T(128)} %constant.8.clone.1), kind=kCustom, calls=%fused_computation.2 | custom fusion | flops 524288 | bytes 4194820 | tf_op jit(solution)/shard_map/scatter-add | solution.py:78
  159.1 4.4 %slice_bitcast_fusion = f32[128,8192]{0,1:T(8,128)} fusion(f32[8193,128]{1,0:T(8,128)} %scatter_custom_fusion), kind=kLoop, calls=%fused_computation.1 | loop fusion | bytes 8388608 | tf_op jit(solution)/shard_map/transpose | solution.py:79
  163.5 5.6 %copy.22 = f32[128,8192]{1,0:T(8,128)} copy(f32[128,8192]{0,1:T(8,128)} %slice_bitcast_fusion) | data formatting | bytes 8388608 | tf_op jit(solution)/shard_map/transpose | solution.py:79
  (24 shorter events, 0.8 us)
Async XLA Ops:
  6.5 36.2 %all-gather.3.cloned.1.call-start = ((), (), s32[]{:S(2)}) async-start(), calls=%async_computation.3 | async-start | bytes 1966080 | tf_op jit(solution)/shard_map/all_gather | solution.py:32
  7.3 68.2 %all-gather.5.cloned.1.call-start = ((), (), s32[]{:S(2)}) async-start(), calls=%async_computation.4 | async-start | bytes 1966080 | tf_op jit(solution)/shard_map/all_gather | solution.py:32
  10.3 2.0 %copy-start.2 = (s32[2048]{0:T(1024)S(1)}, s32[2048]{0:T(1024)}, u32[]{:S(2)}) copy-start(s32[2048]{0:T(1024)} %param.14) | copy-start | bytes 24580
  10.3 2.0 %copy-start = (bf16[1,512,512]{2,1,0:T(8,128)(2,1)S(1)}, bf16[1,512,512]{2,1,0:T(8,128)(2,1)}, u32[]{:S(2)}) copy-start(bf16[1,512,512]{2,1,0:T(8,128)(2,1)} %param.10) | copy-start | bytes 1572868
  10.3 2.0 %copy-start.1 = (bf16[1,512,512]{2,1,0:T(8,128)(2,1)S(1)}, bf16[1,512,512]{2,1,0:T(8,128)(2,1)}, u32[]{:S(2)}) copy-start(bf16[1,512,512]{2,1,0:T(8,128)(2,1)} %param.8) | copy-start | bytes 1572868
  12.1 30.7 %copy-start.4 = (bf16[1,512,512]{2,1,0:T(8,128)(2,1)S(1)}, bf16[1,512,512]{2,1,0:T(8,128)(2,1)}, u32[]{:S(2)}) copy-start(bf16[1,512,512]{2,1,0:T(8,128)(2,1)} %param.9) | copy-start | bytes 1572868
  46.4 29.0 %copy-start.5 = (f32[512,512]{1,0:T(8,128)S(1)}, f32[512,512]{1,0:T(8,128)}, u32[]{:S(2)}) copy-start(f32[512,512]{1,0:T(8,128)} %get-tuple-element.10) | copy-start | bytes 3145732
  77.9 4.4 %copy-start.3 = (s32[64,1]{0,1:T(1,128)S(1)}, s32[64,1]{0,1:T(1,128)}, u32[]{:S(2)}) copy-start(s32[64,1]{0,1:T(1,128)} %param.15) | copy-start | bytes 772
  78.8 11.6 %all-to-all-start.1 = ((bf16[4,128,512]{1,2,0:T(8,128)(2,1)}), bf16[4,128,512]{1,2,0:T(8,128)(2,1)S(1)}, u32[]{:S(2)}, u32[]{:S(2)}) async-start(bf16[4,128,512]{1,2,0:T(8,128)(2,1)} %bitcast.97), calls=%async_computation.1 | async-start | bytes 1048576 | tf_op jit(solution)/shard_map/all_to_all | solution.py:47
  90.4 10.3 %all-to-all-start = ((s32[8,1,512]{2,1,0:T(1,128)}), s32[8,1,512]{2,1,0:T(1,128)S(1)}, u32[]{:S(2)}, u32[]{:S(2)}) async-start(s32[8,1,512]{2,1,0:T(1,128)} %all_to_all.30), calls=%async_computation | async-start | bytes 32768 | tf_op jit(solution)/shard_map/all_to_all | solution.py:74
  100.7 30.1 %all-to-all-start.2 = ((bf16[8,128,512]{1,2,0:T(8,128)(2,1)}), bf16[8,128,512]{1,2,0:T(8,128)(2,1)S(1)}, u32[]{:S(2)}, u32[]{:S(2)}) async-start(bf16[8,128,512]{1,2,0:T(8,128)(2,1)} %bitcast.25), calls=%async_computation.2 | async-start | bytes 2097152 | tf_op jit(solution)/shard_map/all_to_all | solution.py:73
Sparse Core Ops, SparseCore 0:
  9.2 33.5 all-gather.2
  44.6 30.8 all-gather.4
where the time goes:
time: 176 us
  waiting for transfers between devices  97.7 us (56%)
  other arithmetic  32.2 us (18%)
  between operations  14.2 us (8%)
  local copies, waits for them, and re-layouts  13.4 us (8%)
  starting transfers between devices  11.7 us (7%)
  matrix products  6.8 us (4%)
    all_gather x2, waiting for transfers between devices, apply_taps(): lax.all_gather(weights, 'fsdp', axis=1, tiled=True)  58.8 us
    scatter-add x1, other arithmetic, body(): summed = jax.ops.segment_sum(flat_rows, safe_ids, num_segments=ROWS_OWN + 1)  28.2 us
    all_to_all x1, waiting for transfers between devices, body(): lax.all_to_all(send_rows, 'grp', split_axis=0, concat_axis=0, tiled=True)  26.5 us
    transpose x2, local copies, waits for them, and re-layouts, body(): return summed[:ROWS_OWN].T  10 us
    all_to_all x1, waiting for transfers between devices, body(): lax.all_to_all(row_grad.T, 'fsdp', split_axis=0, concat_axis=1, tiled=True)  7.07 us
    dot_general x2, matrix products, apply_taps(): jnp.einsum('ktd,kpd->tp', tap_rows, lax.all_gather(weights, 'fsdp', axis=...  6.08 us
    all_to_all x1, starting transfers between devices, body(): lax.all_to_all(send_ids, 'grp', split_axis=0, concat_axis=0, tiled=True)  4.6 us
    all_to_all x1, waiting for transfers between devices, body(): lax.all_to_all(send_ids, 'grp', split_axis=0, concat_axis=0, tiled=True)  3.93 us
  transfers between devices with their start and end apart: 5, of which 5 were waited for; matrix products, arithmetic and copies ran while one was open for 6% of the time, Pallas kernels for 0%

commit v1 on v0

--- a/solution.py
+++ b/solution.py
@@ -5,6 +5,22 @@
 
 BLK = 32
 ROWS_OWN = 8192
+
+
+def pairwise_exchange(array, axis, split, join):
+    ways, here = (lax.axis_size(axis), lax.axis_index(axis))
+    width = array.shape[split] // ways
+    shape = list(array.shape)
+    shape[split] = width
+    height = shape[join]
+    shape[join] = height * ways
+    full = jnp.zeros(shape, array.dtype)
+    for mask in range(ways):
+        part = lax.dynamic_slice_in_dim(array, (here ^ mask) * width, width, axis=split)
+        if mask:
+            part = lax.ppermute(part, axis, [(d, d ^ mask) for d in range(ways)])
+        full = lax.dynamic_update_slice_in_dim(full, part, (here ^ mask) * height, axis=join)
+    return full
 
 
 def layer_back(gradient, pre_acts, live_rows, dilation, product):
@@ -71,7 +87,7 @@
     send_ids = send_ids.reshape(owner_count, slot_cap * BLK)
     recv_rows, recv_ids = (
         lax.all_to_all(send_rows, "grp", split_axis=0, concat_axis=0, tiled=True),
-        lax.all_to_all(send_ids, "grp", split_axis=0, concat_axis=0, tiled=True),
+        pairwise_exchange(send_ids, "grp", 0, 0),
     )
     flat_rows = jnp.transpose(recv_rows, (0, 2, 1)).reshape(-1, feat_cols).astype(jnp.float32)
     safe_ids = jnp.where(recv_ids < 0, ROWS_OWN, recv_ids).reshape(-1)

time: 176 us -> 170 us (0.966)
  waiting for transfers between devices: 97.7 us -> 87.1 us
  starting transfers between devices: 11.7 us -> 16.8 us
    all_to_all x1, waiting for transfers between devices: 26.5 us -> 0.01 us  [body(): lax.all_to_all(send_rows, 'grp', split_axis=0, concat_axis=0, tiled=True)]
    ppermute x0 -> x7, waiting for transfers between devices: none -> 17.5 us  [pairwise_exchange(): part = lax.ppermute(part, axis, [(d, d ^ mask) for d in range(ways)])]
    ppermute x0 -> x7, starting transfers between devices: none -> 8.61 us  [pairwise_exchange(): part = lax.ppermute(part, axis, [(d, d ^ mask) for d in range(ways)])]
    all_to_all x1 -> x0, starting transfers between devices: 4.6 us -> none  [body(): lax.all_to_all(send_ids, 'grp', split_axis=0, concat_axis=0, tiled=True)]
    all_to_all x1 -> x0, waiting for transfers between devices: 3.93 us -> none  [body(): lax.all_to_all(send_ids, 'grp', split_axis=0, concat_axis=0, tiled=True)]
  transfers between devices with their start and end apart: 5 -> 11, of which waited for: 5 -> 5; matrix products, arithmetic and copies ran while one was open for 6% -> 4% of each run, Pallas kernels for 0% -> 0%
where the time goes in v1:
time: 170 us; the launch traced here: 169 us
  waiting for transfers between devices  87.1 us (51%)
  other arithmetic  30.9 us (18%)
  starting transfers between devices  16.8 us (10%)
  between operations  14.4 us (8%)
  local copies, waits for them, and re-layouts  13.3 us (8%)
  matrix products  6.8 us (4%)
    all_gather x2, waiting for transfers between devices, apply_taps(): lax.all_gather(weights, 'fsdp', axis=1, tiled=True)  60.4 us
    scatter-add x1, other arithmetic, body(): summed = jax.ops.segment_sum(flat_rows, safe_ids, num_segments=ROWS_OWN + 1)  28.2 us
    ppermute x7, waiting for transfers between devices, pairwise_exchange(): part = lax.ppermute(part, axis, [(d, d ^ mask) for d in range(ways)])  17.5 us
    transpose x2, local copies, waits for them, and re-layouts, body(): return summed[:ROWS_OWN].T  10 us
    ppermute x7, starting transfers between devices, pairwise_exchange(): part = lax.ppermute(part, axis, [(d, d ^ mask) for d in range(ways)])  8.61 us
    all_to_all x1, waiting for transfers between devices, body(): lax.all_to_all(row_grad.T, 'fsdp', split_axis=0, concat_axis=1, tiled=True)  7.81 us
    dot_general x2, matrix products, apply_taps(): jnp.einsum('ktd,kpd->tp', tap_rows, lax.all_gather(weights, 'fsdp', axis=...  6.08 us
    all_to_all x1, starting transfers between devices, body(): lax.all_to_all(send_rows, 'grp', split_axis=0, concat_axis=0, tiled=True)  4.73 us
  transfers between devices with their start and end apart: 11, of which 5 were waited for; matrix products, arithmetic and copies ran while one was open for 4% of the time, Pallas kernels for 0%

profile of v1, /device:TPU:0, one launch (start us, length us, event | category | flops | bytes accessed | tf_op | source)
XLA Modules:
  0.0 169.3 jit_solution(3507054277329085984)
XLA Ops:
  6.5 0.7 all-gather.3.cloned.1.call-update
  7.3 0.7 all-gather.5.cloned.1.call-update
  8.7 1.7 %fusion.46 = bf16[512,512]{1,0:T(8,128)(2,1)S(1)} fusion(bf16[1,512,512]{2,1,0:T(8,128)(2,1)} %param.8, bf16[1,512,512]{2,1,0:T(8,128)(2,1)} %param.10), kind=kLoop, calls=%fused_computation.39 | loop fusion | flops 2883584 | bytes 1572864 | tf_op jit(solution)/shard_map/convert_element_type | solution.py:30
  10.8 0.5 fusion.48
  11.2 31.6 %all-gather.3.cloned.1.call-done = bf16[3,512,512]{2,1,0:T(8,128)(2,1)} async-done(((bf16[3,128,512]{2,1,0:T(8,128)(2,1)}), bf16[3,512,512]{2,1,0:T(8,128)(2,1)}) %all-gather.3.cloned.1.call-update) | async-done | bytes 1572880 | tf_op jit(solution)/shard_map/all_gather | solution.py:48
  42.8 3.7 %fusion.54 = (bf16[512,512]{1,0:T(8,128)(2,1)S(1)}, f32[512,512]{1,0:T(8,128)}) fusion(bf16[1,512,512]{2,1,0:T(8,128)(2,1)S(1)} %copy-done.4, bf16[3,512,512]{2,1,0:T(8,128)(2,1)} %all-gather.3.cloned.1.call-done, bf16[1,512,512]{2,1,0:T(8,128)(2,1)S(1)} %get-tuple-element.8, bf16[1,512,512]{2,1,0:T(8,128)(2,1)S(1)} %fusion.48, ...), kind=kOutput, calls=%fused_computation.47 | convolution fusion | flops 810287104 | bytes 5769216 | tf_op jit(solution)/shard_map/ktd,kpd->tp/dot_general | solution.py:45
  46.7 28.8 %all-gather.5.cloned.1.call-done = bf16[3,512,512]{2,1,0:T(8,128)(2,1)} async-done(((bf16[3,128,512]{2,1,0:T(8,128)(2,1)}), bf16[3,512,512]{2,1,0:T(8,128)(2,1)}) %all-gather.5.cloned.1.call-update) | async-done | bytes 1572880 | tf_op jit(solution)/shard_map/all_gather | solution.py:48
  75.5 2.4 %fusion.42 = bf16[64,4,8,128]{3,2,1,0:T(8,128)(2,1)S(1)} fusion(f32[512,512]{1,0:T(8,128)S(1)} %copy-done.5, bf16[3,512,512]{2,1,0:T(8,128)(2,1)} %all-gather.5.cloned.1.call-done, bf16[1,512,512]{2,1,0:T(8,128)(2,1)S(1)} %get-tuple-element.6, bf16[1,512,512]{2,1,0:T(8,128)(2,1)S(1)} %bitcast.102, bf16[1,512,512]{2,1,0:T(8,128)(2,1)S(1)} %get-tuple-element.5, ...), kind=kOutput, calls=%fused_computation.36 | convolution fusion | flops 807927808 | bytes 4720640 | tf_op jit(solution)/shard_map/ktd,kpd->tp/dot_general | solution.py:45
  77.9 0.9 copy.28
  78.8 3.5 %all-to-all-start = ((bf16[4,128,512]{1,2,0:T(8,128)(2,1)}), bf16[4,128,512]{1,2,0:T(8,128)(2,1)S(1)}, u32[]{:S(2)}, u32[]{:S(2)}) async-start(bf16[4,128,512]{1,2,0:T(8,128)(2,1)} %bitcast.98), calls=%async_computation | async-start | bytes 1048576 | tf_op jit(solution)/shard_map/all_to_all | solution.py:63
  82.6 7.8 %all-to-all-done = bf16[4,128,512]{1,2,0:T(8,128)(2,1)S(1)} async-done(((bf16[4,128,512]{1,2,0:T(8,128)(2,1)}), bf16[4,128,512]{1,2,0:T(8,128)(2,1)S(1)}, u32[]{:S(2)}, u32[]{:S(2)}) %all-to-all-start) | async-done | bytes 524320 | tf_op jit(solution)/shard_map/all_to_all | solution.py:63
  90.4 0.5 fusion.14
  90.9 1.2 copy.14
  92.1 4.7 %all-to-all-start.1 = ((bf16[8,128,512]{1,2,0:T(8,128)(2,1)}), bf16[8,128,512]{1,2,0:T(8,128)(2,1)S(1)}, u32[]{:S(2)}, u32[]{:S(2)}) async-start(bf16[8,128,512]{1,2,0:T(8,128)(2,1)} %bitcast.23), calls=%async_computation.1 | async-start | bytes 2097152 | tf_op jit(solution)/shard_map/all_to_all | solution.py:89
  96.9 0.2 convolution_add_fusion
  97.3 2.1 %collective-permute-start.1 = (s32[1,512]{1,0:T(1,128)S(1)}, s32[1,512]{1,0:T(1,128)S(1)}, u32[]{:S(2)}, u32[]{:S(2)}) collective-permute-start(s32[1,512]{1,0:T(1,128)S(1)} %get-tuple-element.14), channel_id=1, source_target_pairs={{0,2},{1,3},{2,0},{3,1},{4,6},{5,7},{6,4},{7,5},{8,10},{9,11},{10,... | collective-permute-start | bytes 6152 | tf_op jit(solution)/shard_map/ppermute | solution.py:21
  99.4 2.5 %collective-permute-start.4 = (s32[1,512]{1,0:T(1,128)S(1)}, s32[1,512]{1,0:T(1,128)S(1)}, u32[]{:S(2)}, u32[]{:S(2)}) collective-permute-start(s32[1,512]{1,0:T(1,128)S(1)} %get-tuple-element.11), channel_id=1, source_target_pairs={{0,5},{1,4},{2,7},{3,6},{4,1},{5,0},{6,3},{7,2},{8,13},{9,12},{10,... | collective-permute-start | bytes 6152 | tf_op jit(solution)/shard_map/ppermute | solution.py:21
  102.1 0.4 collective-permute-start.3
  102.5 12.6 %collective-permute-done.1 = s32[1,512]{1,0:T(1,128)S(1)} collective-permute-done((s32[1,512]{1,0:T(1,128)S(1)}, s32[1,512]{1,0:T(1,128)S(1)}, u32[]{:S(2)}, u32[]{:S(2)}) %collective-permute-start.1) | collective-permute-done | bytes 2080 | tf_op jit(solution)/shard_map/ppermute | solution.py:21
  115.0 3.5 %collective-permute-start.5 = (s32[1,512]{1,0:T(1,128)S(1)}, s32[1,512]{1,0:T(1,128)S(1)}, u32[]{:S(2)}, u32[]{:S(2)}) collective-permute-start(s32[1,512]{1,0:T(1,128)S(1)} %get-tuple-element.10), channel_id=1, source_target_pairs={{0,6},{1,7},{2,4},{3,5},{4,2},{5,3},{6,0},{7,1},{8,14},{9,15},{10,... | collective-permute-start | bytes 6152 | tf_op jit(solution)/shard_map/ppermute | solution.py:21
  118.8 4.9 %collective-permute-done.3 = s32[1,512]{1,0:T(1,128)S(1)} collective-permute-done((s32[1,512]{1,0:T(1,128)S(1)}, s32[1,512]{1,0:T(1,128)S(1)}, u32[]{:S(2)}, u32[]{:S(2)}) %collective-permute-start.3) | collective-permute-done | bytes 2080 | tf_op jit(solution)/shard_map/ppermute | solution.py:21
  124.2 28.2 %scatter_custom_fusion = f32[8193,128]{1,0:T(8,128)} fusion(s32[4096]{0:T(1024)S(1)} %bitcast.103, f32[4096,128]{1,0:T(8,128)S(1)} %bitcast.100, f32[]{:T(128)} %constant.16.clone.1), kind=kCustom, calls=%fused_computation.2 | custom fusion | flops 524288 | bytes 4194820 | tf_op jit(solution)/shard_map/scatter-add | solution.py:94
  152.4 4.4 %slice_bitcast_fusion = f32[128,8192]{0,1:T(8,128)} fusion(f32[8193,128]{1,0:T(8,128)} %scatter_custom_fusion), kind=kLoop, calls=%fused_computation.1 | loop fusion | bytes 8388608 | tf_op jit(solution)/shard_map/transpose | solution.py:95
  156.9 5.6 %copy.15 = f32[128,8192]{1,0:T(8,128)} copy(f32[128,8192]{0,1:T(8,128)} %slice_bitcast_fusion) | data formatting | bytes 8388608 | tf_op jit(solution)/shard_map/transpose | solution.py:95
  (47 shorter events, 1.8 us)
Async XLA Ops:
  6.5 36.2 %all-gather.3.cloned.1.call-start = ((), (), s32[]{:S(2)}) async-start(), calls=%async_computation.2 | async-start | bytes 1966080 | tf_op jit(solution)/shard_map/all_gather | solution.py:48
  7.3 68.2 %all-gather.5.cloned.1.call-start = ((), (), s32[]{:S(2)}) async-start(), calls=%async_computation.3 | async-start | bytes 1966080 | tf_op jit(solution)/shard_map/all_gather | solution.py:48
  8.7 2.0 %copy-start.3 = (s32[64,1]{0,1:T(1,128)S(1)}, s32[64,1]{0,1:T(1,128)}, u32[]{:S(2)}) copy-start(s32[64,1]{0,1:T(1,128)} %param.15) | copy-start | bytes 772
  8.7 2.1 %copy-start = (bf16[1,512,512]{2,1,0:T(8,128)(2,1)S(1)}, bf16[1,512,512]{2,1,0:T(8,128)(2,1)}, u32[]{:S(2)}) copy-start(bf16[1,512,512]{2,1,0:T(8,128)(2,1)} %param.10) | copy-start | bytes 1572868
  8.7 2.1 %copy-start.1 = (bf16[1,512,512]{2,1,0:T(8,128)(2,1)S(1)}, bf16[1,512,512]{2,1,0:T(8,128)(2,1)}, u32[]{:S(2)}) copy-start(bf16[1,512,512]{2,1,0:T(8,128)(2,1)} %param.8) | copy-start | bytes 1572868
  10.4 32.4 %copy-start.4 = (bf16[1,512,512]{2,1,0:T(8,128)(2,1)S(1)}, bf16[1,512,512]{2,1,0:T(8,128)(2,1)}, u32[]{:S(2)}) copy-start(bf16[1,512,512]{2,1,0:T(8,128)(2,1)} %param.9) | copy-start | bytes 1572868
  46.4 29.0 %copy-start.5 = (f32[512,512]{1,0:T(8,128)S(1)}, f32[512,512]{1,0:T(8,128)}, u32[]{:S(2)}) copy-start(f32[512,512]{1,0:T(8,128)} %get-tuple-element.18) | copy-start | bytes 3145732
  78.8 11.6 %all-to-all-start = ((bf16[4,128,512]{1,2,0:T(8,128)(2,1)}), bf16[4,128,512]{1,2,0:T(8,128)(2,1)S(1)}, u32[]{:S(2)}, u32[]{:S(2)}) async-start(bf16[4,128,512]{1,2,0:T(8,128)(2,1)} %bitcast.98), calls=%async_computation | async-start | bytes 1048576 | tf_op jit(solution)/shard_map/all_to_all | solution.py:63
  92.1 4.7 %copy-start.2 = (s32[2048]{0:T(1024)S(1)}, s32[2048]{0:T(1024)}, u32[]{:S(2)}) copy-start(s32[2048]{0:T(1024)} %param.14) | copy-start | bytes 24580
  92.1 31.9 %all-to-all-start.1 = ((bf16[8,128,512]{1,2,0:T(8,128)(2,1)}), bf16[8,128,512]{1,2,0:T(8,128)(2,1)S(1)}, u32[]{:S(2)}, u32[]{:S(2)}) async-start(bf16[8,128,512]{1,2,0:T(8,128)(2,1)} %bitcast.23), calls=%async_computation.1 | async-start | bytes 2097152 | tf_op jit(solution)/shard_map/all_to_all | solution.py:89
  97.3 17.7 %collective-permute-start.1 = (s32[1,512]{1,0:T(1,128)S(1)}, s32[1,512]{1,0:T(1,128)S(1)}, u32[]{:S(2)}, u32[]{:S(2)}) collective-permute-start(s32[1,512]{1,0:T(1,128)S(1)} %get-tuple-element.14), channel_id=1, source_target_pairs={{0,2},{1,3},{2,0},{3,1},{4,6},{5,7},{6,4},{7,5},{8,10},{9,11},{10,... | collective-permute-start | bytes 6152 | tf_op jit(solution)/shard_map/ppermute | solution.py:21
  99.4 19.1 %collective-permute-start = (s32[1,512]{1,0:T(1,128)S(1)}, s32[1,512]{1,0:T(1,128)S(1)}, u32[]{:S(2)}, u32[]{:S(2)}) collective-permute-start(s32[1,512]{1,0:T(1,128)S(1)} %get-tuple-element.15), channel_id=1, source_target_pairs={{0,1},{1,0},{2,3},{3,2},{4,5},{5,4},{6,7},{7,6},{8,9},{9,8},{10,11... | collective-permute-start | bytes 6152 | tf_op jit(solution)/shard_map/ppermute | solution.py:21
  99.4 24.3 %collective-permute-start.4 = (s32[1,512]{1,0:T(1,128)S(1)}, s32[1,512]{1,0:T(1,128)S(1)}, u32[]{:S(2)}, u32[]{:S(2)}) collective-permute-start(s32[1,512]{1,0:T(1,128)S(1)} %get-tuple-element.11), channel_id=1, source_target_pairs={{0,5},{1,4},{2,7},{3,6},{4,1},{5,0},{6,3},{7,2},{8,13},{9,12},{10,... | collective-permute-start | bytes 6152 | tf_op jit(solution)/shard_map/ppermute | solution.py:21
  101.9 16.8 %collective-permute-start.2 = (s32[1,512]{1,0:T(1,128)S(1)}, s32[1,512]{1,0:T(1,128)S(1)}, u32[]{:S(2)}, u32[]{:S(2)}) collective-permute-start(s32[1,512]{1,0:T(1,128)S(1)} %get-tuple-element.13), channel_id=1, source_target_pairs={{0,3},{1,2},{2,1},{3,0},{4,7},{5,6},{6,5},{7,4},{8,11},{9,10},{10,... | collective-permute-start | bytes 6152 | tf_op jit(solution)/shard_map/ppermute | solution.py:21
  102.1 21.6 %collective-permute-start.3 = (s32[1,512]{1,0:T(1,128)S(1)}, s32[1,512]{1,0:T(1,128)S(1)}, u32[]{:S(2)}, u32[]{:S(2)}) collective-permute-start(s32[1,512]{1,0:T(1,128)S(1)} %get-tuple-element.12), channel_id=1, source_target_pairs={{0,4},{1,5},{2,6},{3,7},{4,0},{5,1},{6,2},{7,3},{8,12},{9,13},{10,... | collective-permute-start | bytes 6152 | tf_op jit(solution)/shard_map/ppermute | solution.py:21
  115.0 8.8 %collective-permute-start.5 = (s32[1,512]{1,0:T(1,128)S(1)}, s32[1,512]{1,0:T(1,128)S(1)}, u32[]{:S(2)}, u32[]{:S(2)}) collective-permute-start(s32[1,512]{1,0:T(1,128)S(1)} %get-tuple-element.10), channel_id=1, source_target_pairs={{0,6},{1,7},{2,4},{3,5},{4,2},{5,3},{6,0},{7,1},{8,14},{9,15},{10,... | collective-permute-start | bytes 6152 | tf_op jit(solution)/shard_map/ppermute | solution.py:21
  118.5 5.4 %collective-permute-start.6 = (s32[1,512]{1,0:T(1,128)S(1)}, s32[1,512]{1,0:T(1,128)S(1)}, u32[]{:S(2)}, u32[]{:S(2)}) collective-permute-start(s32[1,512]{1,0:T(1,128)S(1)} %get-tuple-element.9), channel_id=1, source_target_pairs={{0,7},{1,6},{2,5},{3,4},{4,3},{5,2},{6,1},{7,0},{8,15},{9,14},{10,... | collective-permute-start | bytes 6152 | tf_op jit(solution)/shard_map/ppermute | solution.py:21
Sparse Core Ops, SparseCore 0:
  9.2 33.5 all-gather.2
  44.6 30.8 all-gather.4
